TPU v7x, 32 devices: a whole 2x2x4 slice. The times are simulated.
32 devices in a mesh: layer: 16 (over z, x, core), dp: 2 (over y).
Axes of the slice: x: 2, y: 2, z: 4, core: 2. Of those that a mesh axis runs over, the one named last changes fastest.
Arguments:
- weights: float32 [32, 1024, 1024], P('layer', 'dp'), may hold values from -6 to 6
- momentum: float32 [32, 1024, 1024], P('layer', 'dp'), may hold values from -3 to 3
- boundary: float32 [16, 512, 1024], P('layer', 'dp'), may hold values from -6 to 6
- adjoint: float32 [16, 512, 1024], P('layer', 'dp'), may hold values from -6 to 6
- target: float32 [512, 1024], P('dp'), may hold values from -6 to 6
Outputs:
- new_weights: float32 [32, 1024, 1024], P('layer', 'dp')
- new_momentum: float32 [32, 1024, 1024], P('layer', 'dp')
- new_boundary: float32 [16, 512, 1024], P('layer', 'dp')
- new_adjoint: float32 [16, 512, 1024], P('layer', 'dp')
All inputs are finite; a program needn't handle non-finite values.
Results may differ from a plain program's by a relative error of at most 0.012.
Values may be sent and summed in bfloat16 or wider, within the bound.
A program may use at most 64 MiB of HBM per device.

v0:
```python
import math
import jax
import jax.numpy as jnp
from jax import lax
from jax.sharding import PartitionSpec as P

STEPS = 2
SWEEPS = 2
step_size = 0.5
momentum_decay = 0.9
learn_rate = 0.05


def passed_along(value, axis, by):
    devices = lax.axis_size(axis)
    pairs = [(i, i + by) for i in range(devices) if 0 <= i + by < devices]
    return lax.ppermute(value, axis, pairs)


def forward_group(current, full_weights, width_scale):
    inputs_list = []
    slopes_list = []
    for layer_at in range(full_weights.shape[0]):
        rounded = current.astype(jnp.bfloat16)
        product = jnp.dot(rounded, full_weights[layer_at], preferred_element_type=jnp.float32)
        squashed = jnp.tanh(product * width_scale)
        current = current + step_size * squashed
        inputs_list.append(rounded)
        slopes_list.append(squashed)
    return (current, inputs_list, slopes_list)


def pull_back(signal, matrix):
    return lax.dot_general(
        signal, matrix, (((1,), (1,)), ((), ())), preferred_element_type=jnp.float32
    )


def backward_group(cotangent, full_weights, slopes_list, width_scale):
    for layer_at in reversed(range(len(slopes_list))):
        slope = slopes_list[layer_at]
        signal = (cotangent * (1.0 - slope * slope)).astype(jnp.bfloat16)
        cotangent = cotangent + step_size * width_scale * pull_back(signal, full_weights[layer_at])
    return cotangent


def outer_rows(left, right):
    return lax.dot_general(
        left, right, (((0,), (0,)), ((), ())), preferred_element_type=jnp.float32
    )


def local(weights, momentum, boundary, adjoint, target):
    groups = lax.axis_size("layer")
    group_at = lax.axis_index("layer")
    shards = lax.axis_size("dp")
    shard_at = lax.axis_index("dp")
    width = weights.shape[2]
    own_rows = weights.shape[1]
    width_scale = 1.0 / math.sqrt(width)
    row_scale = 1.0 / math.sqrt(boundary.shape[1] * shards)
    is_first = group_at == 0
    is_last = group_at == groups - 1
    current_in = boundary[0]
    cotangent_in = adjoint[0]
    for update_at in range(STEPS):
        full_weights = lax.all_gather(weights.astype(jnp.bfloat16), "dp", axis=1, tiled=True)
        for sweep_at in range(SWEEPS):
            outgoing = forward_group(current_in, full_weights, width_scale)[0]
            received = passed_along(outgoing, "layer", 1)
            current_in = jnp.where(is_first, current_in, received)
        finals, inputs_list, slopes_list = forward_group(current_in, full_weights, width_scale)
        missing = finals - target
        for sweep_at in range(SWEEPS):
            starting = backward_group(cotangent_in, full_weights, slopes_list, width_scale)
            received = passed_along(starting, "layer", -1)
            cotangent_in = jnp.where(is_last, missing, received)
        cotangent = cotangent_in
        grads = [None] * len(slopes_list)
        for layer_at in reversed(range(len(slopes_list))):
            slope = slopes_list[layer_at]
            signal = (cotangent * (1.0 - slope * slope)).astype(jnp.bfloat16)
            layer_input = inputs_list[layer_at]
            columns = lax.dynamic_slice_in_dim(
                lax.all_gather(layer_input, "dp", axis=0, tiled=True),
                shard_at * own_rows,
                own_rows,
                1,
            )
            summed = outer_rows(columns, lax.all_gather(signal, "dp", axis=0, tiled=True))
            grads[layer_at] = summed * row_scale
            if layer_at > 0:
                cotangent = cotangent + step_size * width_scale * pull_back(
                    signal, full_weights[layer_at]
                )
        momentum = momentum_decay * momentum + jnp.stack(grads, axis=0)
        weights = weights - learn_rate * momentum
    return (weights, momentum, current_in[None], cotangent_in[None])


def solution(mesh):
    placed = (
        P("layer", "dp", None),
        P("layer", "dp", None),
        P("layer", "dp", None),
        P("layer", "dp", None),
        P("dp", None),
    )
    return jax.shard_map(
        local,
        mesh=mesh,
        in_specs=placed,
        out_specs=(
            P("layer", "dp", None),
            P("layer", "dp", None),
            P("layer", "dp", None),
            P("layer", "dp", None),
        ),
        check_vma=False,
    )
```

profile of v0, /device:TPU:0, one launch (start us, length us, event | category | flops | bytes accessed | tf_op | source)
XLA Modules:
  0.0 482.2 jit_solution(8640510637645091248)
XLA Ops:
  7.2 3.9 convert_element_type.81
  11.2 59.6 %all-gather.11.cloned.1.call-done = bf16[2,1024,1024]{2,1,0:T(8,128)(2,1)} async-done(((bf16[2,512,1024]{2,1,0:T(8,128)(2,1)}), bf16[2,1024,1024]{2,1,0:T(8,128)(2,1)}) %all-gather.11.cloned.1.call-update) | async-done | bytes 4194320 | tf_op jit(solution)/shard_map/all_gather | solution.py:67
  70.8 2.5 fusion.40
  73.2 0.3 copy-done
  73.6 0.7 fusion.37
  74.3 1.6 collective-permute-start
  76.0 2.2 collective-permute-done
  78.2 2.8 fusion.34
  81.0 0.8 fusion.31
  81.7 13.3 %collective-permute-start.1 = (f32[256,1024]{1,0:T(8,128)S(1)}, f32[256,1024]{1,0:T(8,128)S(1)}, u32[]{:S(2)}, u32[]{:S(2)}) collective-permute-start(f32[256,1024]{1,0:T(8,128)S(1)} %fusion.31), channel_id=1, source_target_pairs={{0,2},{2,4},{4,6},{6,8},{8,10},{10,12},{12,14},{14,16},{16,18},{18... | collective-permute-start | bytes 3145736 | tf_op jit(solution)/shard_map/ppermute | solution.py:17
  95.1 2.2 collective-permute-done.1
  97.6 3.3 fusion.69
  101.0 3.0 add_subtract_fusion.1
  104.5 0.7 fusion.26
  105.3 1.8 fusion.25
  107.1 1.3 collective-permute-start.2
  108.4 16.2 %collective-permute-done.2 = f32[256,1024]{1,0:T(8,128)} collective-permute-done((f32[256,1024]{1,0:T(8,128)}, f32[256,1024]{1,0:T(8,128)}, u32[]{:S(2)}, u32[]{:S(2)}) %collective-permute-start.2) | collective-permute-done | bytes 1048608 | tf_op jit(solution)/shard_map/ppermute | solution.py:17
  124.6 3.3 fusion.24
  127.9 1.8 fusion.23
  129.7 1.3 collective-permute-start.3
  131.0 15.8 %collective-permute-done.3 = f32[256,1024]{1,0:T(8,128)} collective-permute-done((f32[256,1024]{1,0:T(8,128)}, f32[256,1024]{1,0:T(8,128)}, u32[]{:S(2)}, u32[]{:S(2)}) %collective-permute-start.3) | collective-permute-done | bytes 1048608 | tf_op jit(solution)/shard_map/ppermute | solution.py:17
  146.8 2.7 multiply_convert_fusion.9
  149.5 3.7 fusion.41
  153.3 0.5 all-gather.17.cloned.1.call-update
  153.8 0.5 all-gather.19.cloned.1.call-update
  154.6 13.2 %all-gather.13.cloned.1.call-done = bf16[512,1024]{1,0:T(8,128)(2,1)} async-done(((bf16[256,1024]{1,0:T(8,128)(2,1)}), bf16[512,1024]{1,0:T(8,128)(2,1)}) %all-gather.13.cloned.1.call-update) | async-done | bytes 1048592 | tf_op jit(solution)/shard_map/all_gather | solution.py:85
  167.8 23.4 %all-gather.15.cloned.1.call-done = bf16[512,1024]{1,0:T(8,128)(2,1)} async-done(((bf16[256,1024]{1,0:T(8,128)(2,1)}), bf16[512,1024]{1,0:T(8,128)(2,1)}) %all-gather.15.cloned.1.call-update) | async-done | bytes 1048592 | tf_op jit(solution)/shard_map/all_gather | solution.py:90
  191.2 3.4 multiply_bitcast_fusion.3
  194.6 19.9 %all-gather.17.cloned.1.call-done = bf16[512,1024]{1,0:T(8,128)(2,1)} async-done(((bf16[256,1024]{1,0:T(8,128)(2,1)}), bf16[512,1024]{1,0:T(8,128)(2,1)}) %all-gather.17.cloned.1.call-update) | async-done | bytes 1048592 | tf_op jit(solution)/shard_map/all_gather | solution.py:85
  214.5 23.3 %all-gather.19.cloned.1.call-done = bf16[512,1024]{1,0:T(8,128)(2,1)} async-done(((bf16[256,1024]{1,0:T(8,128)(2,1)}), bf16[512,1024]{1,0:T(8,128)(2,1)}) %all-gather.19.cloned.1.call-update) | async-done | bytes 1048592 | tf_op jit(solution)/shard_map/all_gather | solution.py:90
  237.8 2.3 multiply_bitcast_fusion.2
  240.1 1.4 copy-done.13
  241.4 5.8 %fusion = bf16[2,512,1024]{2,1,0:T(8,128)(2,1)} fusion(f32[2,512,1024]{2,1,0:T(8,128)S(1)} %copy-done.6, f32[1,512,1024]{2,1,0:T(8,128)S(1)} %multiply_bitcast_fusion.2, f32[1,512,1024]{2,1,0:T(8,128)} %multiply_bitcast_fusion.3, f32[2,512,1024]{2,1,0:T(8,128)} %param.6), kind=kLoop, calls=%fused_computation.12 | loop fusion | flops 6291456 | bytes 14680064 | tf_op jit(solution)/shard_map/convert_element_type | solution.py:67
  247.3 56.8 %all-gather.21.cloned.1.call-done = bf16[2,1024,1024]{2,1,0:T(8,128)(2,1)} async-done(((bf16[2,512,1024]{2,1,0:T(8,128)(2,1)}), bf16[2,1024,1024]{2,1,0:T(8,128)(2,1)}) %all-gather.21.cloned.1.call-update) | async-done | bytes 4194320 | tf_op jit(solution)/shard_map/all_gather | solution.py:67
  304.1 2.5 fusion.20
  307.0 0.8 fusion.17
  307.7 1.6 collective-permute-start.4
  309.4 2.2 collective-permute-done.4
  311.6 0.9 fusion.14
  312.5 0.8 fusion.11
  313.2 13.3 %collective-permute-start.5 = (f32[256,1024]{1,0:T(8,128)S(1)}, f32[256,1024]{1,0:T(8,128)S(1)}, u32[]{:S(2)}, u32[]{:S(2)}) collective-permute-start(f32[256,1024]{1,0:T(8,128)S(1)} %fusion.11), channel_id=1, source_target_pairs={{0,2},{2,4},{4,6},{6,8},{8,10},{10,12},{12,14},{14,16},{16,18},{18... | collective-permute-start | bytes 3145736 | tf_op jit(solution)/shard_map/ppermute | solution.py:17
  326.6 2.2 collective-permute-done.5
  328.8 1.1 fusion.84
  329.9 3.7 fusion.70
  333.6 3.3 add_subtract_fusion
  337.2 2.5 fusion.6
  339.6 0.8 fusion.5
  340.4 1.3 collective-permute-start.6
  341.7 14.7 %collective-permute-done.6 = f32[256,1024]{1,0:T(8,128)S(1)} collective-permute-done((f32[256,1024]{1,0:T(8,128)S(1)}, f32[256,1024]{1,0:T(8,128)S(1)}, u32[]{:S(2)}, u32[]{:S(2)}) %collective-permute-start.6) | collective-permute-done | bytes 1048608 | tf_op jit(solution)/shard_map/ppermute | solution.py:17
  356.4 0.9 fusion.4
  357.3 1.8 fusion.3
  359.1 1.3 collective-permute-start.7
  360.4 15.8 %collective-permute-done.7 = f32[256,1024]{1,0:T(8,128)} collective-permute-done((f32[256,1024]{1,0:T(8,128)}, f32[256,1024]{1,0:T(8,128)}, u32[]{:S(2)}, u32[]{:S(2)}) %collective-permute-start.7) | collective-permute-done | bytes 1048608 | tf_op jit(solution)/shard_map/ppermute | solution.py:17
  376.3 2.7 fusion.71
  379.0 3.7 fusion.42
  382.8 0.7 all-gather.27.cloned.1.call-update
  384.1 13.1 %all-gather.23.cloned.1.call-done = bf16[512,1024]{1,0:T(8,128)(2,1)} async-done(((bf16[256,1024]{1,0:T(8,128)(2,1)}), bf16[512,1024]{1,0:T(8,128)(2,1)}) %all-gather.23.cloned.1.call-update) | async-done | bytes 1048592 | tf_op jit(solution)/shard_map/all_gather | solution.py:85
  397.2 22.9 %all-gather.25.cloned.1.call-done = bf16[512,1024]{1,0:T(8,128)(2,1)} async-done(((bf16[256,1024]{1,0:T(8,128)(2,1)}), bf16[512,1024]{1,0:T(8,128)(2,1)}) %all-gather.25.cloned.1.call-update) | async-done | bytes 1048592 | tf_op jit(solution)/shard_map/all_gather | solution.py:90
  420.1 3.5 multiply_bitcast_fusion.1
  423.5 19.4 %all-gather.27.cloned.1.call-done = bf16[512,1024]{1,0:T(8,128)(2,1)} async-done(((bf16[256,1024]{1,0:T(8,128)(2,1)}), bf16[512,1024]{1,0:T(8,128)(2,1)}) %all-gather.27.cloned.1.call-update) | async-done | bytes 1048592 | tf_op jit(solution)/shard_map/all_gather | solution.py:85
  442.9 23.3 %all-gather.29.cloned.1.call-done = bf16[512,1024]{1,0:T(8,128)(2,1)} async-done(((bf16[256,1024]{1,0:T(8,128)(2,1)}), bf16[512,1024]{1,0:T(8,128)(2,1)}) %all-gather.29.cloned.1.call-update) | async-done | bytes 1048592 | tf_op jit(solution)/shard_map/all_gather | solution.py:90
  466.2 2.3 multiply_bitcast_fusion
  468.5 0.4 copy-done.7
  468.9 6.5 %multiply_subtract_fusion = (f32[2,512,1024]{2,1,0:T(8,128)}, f32[2,512,1024]{2,1,0:T(8,128)}) fusion(f32[2,512,1024]{2,1,0:T(8,128)S(1)} %copy-done.7, f32[1,512,1024]{2,1,0:T(8,128)} %copy-done.13, f32[1,512,1024]{2,1,0:T(8,128)S(1)} %copy-done.12, f32[2,512,1024]{2,1,0:T(8,128)} %param.6, f32[1,512,1024]{2,1,0:T(8,128)S(1)} %multiply_bitcast_fusion, ...), kind=kLoop, calls=%fused_computation.2 | loop fusion | flops 10485760 | bytes 25165824 | tf_op jit(solution)/shard_map/sub | solution.py:97
  (53 shorter events, 2.8 us)
Async XLA Ops:
  7.2 63.6 %copy-start.16 = (f32[1,256,1024]{2,1,0:T(8,128)S(1)}, f32[1,256,1024]{2,1,0:T(8,128)}, u32[]{:S(2)}) copy-start(f32[1,256,1024]{2,1,0:T(8,128)} %param.7) | copy-start | bytes 3145732
  7.2 63.6 %all-gather.11.cloned.1.call-start = ((), (), s32[]{:S(2)}) async-start(), calls=%async_computation | async-start | bytes 6291456 | tf_op jit(solution)/shard_map/all_gather | solution.py:67
  11.2 156.6 %all-gather.13.cloned.1.call-start = ((), (), s32[]{:S(2)}) async-start(), calls=%async_computation.1 | async-start | bytes 1572864 | tf_op jit(solution)/shard_map/all_gather | solution.py:85
  70.8 2.8 copy-start
  74.3 3.9 collective-permute-start
  76.0 5.0 %copy-start.1 = (bf16[2,1024,1024]{2,1,0:T(8,128)(2,1)S(1)}, bf16[2,1024,1024]{2,1,0:T(8,128)(2,1)}, u32[]{:S(2)}) copy-start(bf16[2,1024,1024]{2,1,0:T(8,128)(2,1)} %all-gather.11.cloned.1.call-done) | copy-start | bytes 12582916
  78.2 3.6 copy-start.18
  81.7 15.5 %collective-permute-start.1 = (f32[256,1024]{1,0:T(8,128)S(1)}, f32[256,1024]{1,0:T(8,128)S(1)}, u32[]{:S(2)}, u32[]{:S(2)}) collective-permute-start(f32[256,1024]{1,0:T(8,128)S(1)} %fusion.31), channel_id=1, source_target_pairs={{0,2},{2,4},{4,6},{6,8},{8,10},{10,12},{12,14},{14,16},{16,18},{18... | collective-permute-start | bytes 3145736 | tf_op jit(solution)/shard_map/ppermute | solution.py:17
  97.6 3.3 copy-start.14
  101.0 3.3 copy-start.2
  101.0 3.6 copy-start.17
  104.0 3.1 copy-start.10
  107.1 17.6 %collective-permute-start.2 = (f32[256,1024]{1,0:T(8,128)}, f32[256,1024]{1,0:T(8,128)}, u32[]{:S(2)}, u32[]{:S(2)}) collective-permute-start(f32[256,1024]{1,0:T(8,128)} %fusion.25), channel_id=1, source_target_pairs={{2,0},{4,2},{6,4},{8,6},{10,8},{12,10},{14,12},{16,14},{18,16},{20... | collective-permute-start | bytes 3145736 | tf_op jit(solution)/shard_map/ppermute | solution.py:17
  108.4 19.5 %copy-start.3 = (bf16[2,1024,1024]{2,1,0:T(8,128)(2,1)S(1)}, bf16[2,1024,1024]{2,1,0:T(8,128)(2,1)}, u32[]{:S(2)}) copy-start(bf16[2,1024,1024]{2,1,0:T(8,128)(2,1)} %all-gather.11.cloned.1.call-done) | copy-start | bytes 12582916
  129.7 17.2 %collective-permute-start.3 = (f32[256,1024]{1,0:T(8,128)}, f32[256,1024]{1,0:T(8,128)}, u32[]{:S(2)}, u32[]{:S(2)}) collective-permute-start(f32[256,1024]{1,0:T(8,128)} %fusion.23), channel_id=1, source_target_pairs={{2,0},{4,2},{6,4},{8,6},{10,8},{12,10},{14,12},{16,14},{18,16},{20... | collective-permute-start | bytes 3145736 | tf_op jit(solution)/shard_map/ppermute | solution.py:17
  131.0 60.2 %all-gather.15.cloned.1.call-start = ((), (), s32[]{:S(2)}) async-start(), calls=%async_computation.2 | async-start | bytes 1572864 | tf_op jit(solution)/shard_map/all_gather | solution.py:90
  153.2 61.3 %all-gather.17.cloned.1.call-start = ((), (), s32[]{:S(2)}) async-start(), calls=%async_computation.3 | async-start | bytes 1572864 | tf_op jit(solution)/shard_map/all_gather | solution.py:85
  153.8 84.0 %all-gather.19.cloned.1.call-start = ((), (), s32[]{:S(2)}) async-start(), calls=%async_computation.4 | async-start | bytes 1572864 | tf_op jit(solution)/shard_map/all_gather | solution.py:90
  154.4 149.8 %all-gather.21.cloned.1.call-start = ((), (), s32[]{:S(2)}) async-start(), calls=%async_computation.5 | async-start | bytes 6291456 | tf_op jit(solution)/shard_map/all_gather | solution.py:67
  237.8 3.6 copy-start.6
  240.0 1.4 copy-start.13
  241.4 62.7 %copy-start.15 = (bf16[256,1024]{1,0:T(8,128)(2,1)S(1)}, bf16[256,1024]{1,0:T(8,128)(2,1)}, u32[]{:S(2)}) copy-start(bf16[256,1024]{1,0:T(8,128)(2,1)} %copy-done.14) | copy-start | bytes 1572868
  247.3 149.9 %all-gather.23.cloned.1.call-start = ((), (), s32[]{:S(2)}) async-start(), calls=%async_computation.6 | async-start | bytes 1572864 | tf_op jit(solution)/shard_map/all_gather | solution.py:85
  304.1 2.8 copy-start.4
  307.7 3.9 collective-permute-start.4
  313.2 15.6 %collective-permute-start.5 = (f32[256,1024]{1,0:T(8,128)S(1)}, f32[256,1024]{1,0:T(8,128)S(1)}, u32[]{:S(2)}, u32[]{:S(2)}) collective-permute-start(f32[256,1024]{1,0:T(8,128)S(1)} %fusion.11), channel_id=1, source_target_pairs={{0,2},{2,4},{4,6},{6,8},{8,10},{10,12},{12,14},{14,16},{16,18},{18... | collective-permute-start | bytes 3145736 | tf_op jit(solution)/shard_map/ppermute | solution.py:17
  329.9 3.7 copy-start.11
  333.6 3.6 copy-start.5
  336.9 19.6 %copy-start.8 = (f32[256,1024]{1,0:T(8,128)}, f32[256,1024]{1,0:T(8,128)S(1)}, u32[]{:S(2)}) copy-start(f32[256,1024]{1,0:T(8,128)S(1)} %get-tuple-element.19) | copy-start | bytes 3145732
  340.4 16.0 %collective-permute-start.6 = (f32[256,1024]{1,0:T(8,128)S(1)}, f32[256,1024]{1,0:T(8,128)S(1)}, u32[]{:S(2)}, u32[]{:S(2)}) collective-permute-start(f32[256,1024]{1,0:T(8,128)S(1)} %fusion.5), channel_id=1, source_target_pairs={{2,0},{4,2},{6,4},{8,6},{10,8},{12,10},{14,12},{16,14},{18,16},{20... | collective-permute-start | bytes 3145736 | tf_op jit(solution)/shard_map/ppermute | solution.py:17
  357.3 19.0 %copy-start.9 = (f32[256,1024]{1,0:T(8,128)S(1)}, f32[256,1024]{1,0:T(8,128)}, u32[]{:S(2)}) copy-start(f32[256,1024]{1,0:T(8,128)} %copy-done.8) | copy-start | bytes 3145732
  359.1 17.2 %collective-permute-start.7 = (f32[256,1024]{1,0:T(8,128)}, f32[256,1024]{1,0:T(8,128)}, u32[]{:S(2)}, u32[]{:S(2)}) collective-permute-start(f32[256,1024]{1,0:T(8,128)} %fusion.3), channel_id=1, source_target_pairs={{2,0},{4,2},{6,4},{8,6},{10,8},{12,10},{14,12},{16,14},{18,16},{20... | collective-permute-start | bytes 3145736 | tf_op jit(solution)/shard_map/ppermute | solution.py:17
  360.4 59.7 %all-gather.25.cloned.1.call-start = ((), (), s32[]{:S(2)}) async-start(), calls=%async_computation.7 | async-start | bytes 1572864 | tf_op jit(solution)/shard_map/all_gather | solution.py:90
  382.7 60.2 %all-gather.27.cloned.1.call-start = ((), (), s32[]{:S(2)}) async-start(), calls=%async_computation.8 | async-start | bytes 1572864 | tf_op jit(solution)/shard_map/all_gather | solution.py:85
  383.5 82.7 %all-gather.29.cloned.1.call-start = ((), (), s32[]{:S(2)}) async-start(), calls=%async_computation.9 | async-start | bytes 1572864 | tf_op jit(solution)/shard_map/all_gather | solution.py:90
  384.1 84.4 %copy-start.12 = (f32[1,512,1024]{2,1,0:T(8,128)S(1)}, f32[1,512,1024]{2,1,0:T(8,128)}, u32[]{:S(2)}) copy-start(f32[1,512,1024]{2,1,0:T(8,128)} %multiply_bitcast_fusion.3) | copy-start | bytes 6291460
  466.2 2.7 copy-start.7
Sparse Core Ops, SparseCore 0:
  11.3 59.4 all-gather.10
  131.1 36.6 all-gather.12
  169.9 21.2 all-gather.14
  193.2 21.2 all-gather.16
  216.5 21.2 all-gather.18
  247.4 56.7 all-gather.20
  360.5 36.6 all-gather.22
  398.8 21.2 all-gather.24
  421.6 21.2 all-gather.26
  444.9 21.2 all-gather.28
where the time goes:
time: 483 us; the launch traced here: 482 us
  waiting for transfers between devices  348 us (72%)
  matrix products  57.1 us (12%)
  starting transfers between devices  35.9 us (7%)
  other arithmetic  23.1 us (5%)
  between operations  14.5 us (3%)
    all_gather x2, waiting for transfers between devices, local(): lax.all_gather(weights.astype(jnp.bfloat16), 'dp', axis=1, tiled=True)  116 us
    all_gather x4, waiting for transfers between devices, local(): lax.all_gather(signal, 'dp', axis=0, tiled=True)  92.9 us
    ppermute x8, waiting for transfers between devices, passed_along(): return lax.ppermute(value, axis, pairs)  71.4 us
    all_gather x4, waiting for transfers between devices, local(): lax.all_gather(layer_input, 'dp', axis=0, tiled=True)  65.5 us
    ppermute x8, starting transfers between devices, passed_along(): return lax.ppermute(value, axis, pairs)  35.1 us
    dot_general x12, matrix products, forward_group(): jnp.dot(rounded, full_weights[layer_at], preferred_element_type=jnp.float32)  24.8 us
    dot_general x10, matrix products, pull_back(): lax.dot_general(signal, matrix, (((1,), (1,)), ((), ())), preferred_eleme...  20.8 us
    dot_general x4, matrix products, outer_rows(): lax.dot_general(left, right, (((0,), (0,)), ((), ())), preferred_element_...  11.4 us
  transfers between devices with their start and end apart: 18, of which 18 were waited for; matrix products, arithmetic and copies ran while one was open for 4% of the time, Pallas kernels for 0%

commit v1 on v0

--- a/solution.py
+++ b/solution.py
@@ -9,6 +9,28 @@
 step_size = 0.5
 momentum_decay = 0.9
 learn_rate = 0.05
+
+
+def laid_out(pieces, dim):
+    shape = list(pieces.shape[1:])
+    shape[dim] *= pieces.shape[0]
+    return jnp.moveaxis(pieces, 0, dim).reshape(shape)
+
+
+def grow_blocks(shard, axis):
+    count = lax.axis_size(axis)
+    blocks = shard[None]
+    for level in range(count.bit_length() - 1):
+        bit = 1 << level
+        theirs = lax.ppermute(blocks, axis, [(i, i ^ bit) for i in range(count)])
+        both = jnp.stack([blocks, theirs])
+        upper = lax.axis_index(axis) >> level & 1
+        blocks = jnp.where(upper == 0, both, both[::-1]).reshape(-1, *shard.shape)
+    return blocks
+
+
+def collect(x, axis, dim):
+    return laid_out(grow_blocks(x, axis), dim)
 
 
 def passed_along(value, axis, by):
@@ -87,7 +109,7 @@
                 own_rows,
                 1,
             )
-            summed = outer_rows(columns, lax.all_gather(signal, "dp", axis=0, tiled=True))
+            summed = outer_rows(columns, collect(signal, "dp", 0))
             grads[layer_at] = summed * row_scale
             if layer_at > 0:
                 cotangent = cotangent + step_size * width_scale * pull_back(

time: 483 us -> 409 us (0.85)
  waiting for transfers between devices: 348 us -> 262 us
  other arithmetic: 23.1 us -> 30.9 us
    all_gather x4 -> x0, waiting for transfers between devices: 92.9 us -> none  [local(): lax.all_gather(signal, 'dp', axis=0, tiled=True)]
    ppermute x0 -> x4, waiting for transfers between devices: none -> 50.5 us  [grow_blocks(): theirs = lax.ppermute(blocks, axis, [(i, i ^ bit) for i in range(count)])]
    all_gather x4, waiting for transfers between devices: 65.5 us -> 23.1 us  [local(): lax.all_gather(layer_input, 'dp', axis=0, tiled=True)]
  transfers between devices with their start and end apart: 18 -> 18, of which waited for: 18 -> 16; matrix products, arithmetic and copies ran while one was open for 4% -> 6% of each run, Pallas kernels for 0% -> 0%
where the time goes in v1:
time: 409 us; the launch traced here: 407 us
  waiting for transfers between devices  262 us (64%)
  matrix products  55.4 us (14%)
  starting transfers between devices  39.9 us (10%)
  other arithmetic  30.9 us (8%)
  between operations  14.5 us (4%)
  local copies, waits for them, and re-layouts  4.14 us (1%)
    all_gather x2, waiting for transfers between devices, local(): lax.all_gather(weights.astype(jnp.bfloat16), 'dp', axis=1, tiled=True)  117 us
    ppermute x8, waiting for transfers between devices, passed_along(): return lax.ppermute(value, axis, pairs)  71.1 us
    ppermute x4, waiting for transfers between devices, grow_blocks(): theirs = lax.ppermute(blocks, axis, [(i, i ^ bit) for i in range(count)])  50.5 us
    ppermute x8, starting transfers between devices, passed_along(): return lax.ppermute(value, axis, pairs)  35.1 us
    dot_general x12, matrix products, forward_group(): jnp.dot(rounded, full_weights[layer_at], preferred_element_type=jnp.float32)  24.8 us
    all_gather x4, waiting for transfers between devices, local(): lax.all_gather(layer_input, 'dp', axis=0, tiled=True)  23.1 us
    dot_general x10, matrix products, pull_back(): lax.dot_general(signal, matrix, (((1,), (1,)), ((), ())), preferred_eleme...  19.4 us
    dot_general x4, matrix products, outer_rows(): lax.dot_general(left, right, (((0,), (0,)), ((), ())), preferred_element_...  11.2 us
  transfers between devices with their start and end apart: 18, of which 16 were waited for; matrix products, arithmetic and copies ran while one was open for 6% of the time, Pallas kernels for 0%

profile of v1, /device:TPU:0, one launch (start us, length us, event | category | flops | bytes accessed | tf_op | source)
XLA Modules:
  0.0 407.0 jit_solution(9841727404903846296)
XLA Ops:
  7.2 3.9 convert_element_type.81
  11.2 59.6 %all-gather.7.cloned.1.call-done = bf16[2,1024,1024]{2,1,0:T(8,128)(2,1)} async-done(((bf16[2,512,1024]{2,1,0:T(8,128)(2,1)}), bf16[2,1024,1024]{2,1,0:T(8,128)(2,1)}) %all-gather.7.cloned.1.call-update) | async-done | bytes 4194320 | tf_op jit(solution)/shard_map/all_gather | solution.py:89
  70.8 2.5 fusion.40
  74.3 1.6 collective-permute-start
  76.0 2.2 collective-permute-done
  78.2 2.8 fusion.34
  81.0 0.8 fusion.31
  81.7 13.3 %collective-permute-start.1 = (f32[256,1024]{1,0:T(8,128)S(1)}, f32[256,1024]{1,0:T(8,128)S(1)}, u32[]{:S(2)}, u32[]{:S(2)}) collective-permute-start(f32[256,1024]{1,0:T(8,128)S(1)} %fusion.31), channel_id=1, source_target_pairs={{0,2},{2,4},{4,6},{6,8},{8,10},{10,12},{12,14},{14,16},{16,18},{18... | collective-permute-start | bytes 3145736 | tf_op jit(solution)/shard_map/ppermute | solution.py:39
  95.1 2.2 collective-permute-done.1
  97.6 3.3 fusion.69
  101.0 3.0 add_subtract_fusion.1
  105.3 1.8 fusion.25
  107.1 1.3 collective-permute-start.2
  108.4 16.2 %collective-permute-done.2 = f32[256,1024]{1,0:T(8,128)} collective-permute-done((f32[256,1024]{1,0:T(8,128)}, f32[256,1024]{1,0:T(8,128)}, u32[]{:S(2)}, u32[]{:S(2)}) %collective-permute-start.2) | collective-permute-done | bytes 1048608 | tf_op jit(solution)/shard_map/ppermute | solution.py:39
  124.6 3.3 fusion.24
  127.9 1.8 fusion.23
  129.7 1.3 collective-permute-start.3
  131.0 15.8 %collective-permute-done.3 = f32[256,1024]{1,0:T(8,128)} collective-permute-done((f32[256,1024]{1,0:T(8,128)}, f32[256,1024]{1,0:T(8,128)}, u32[]{:S(2)}, u32[]{:S(2)}) %collective-permute-start.3) | collective-permute-done | bytes 1048608 | tf_op jit(solution)/shard_map/ppermute | solution.py:39
  146.8 2.7 multiply_convert_fusion.9
  150.1 3.7 fusion.41
  153.8 1.5 collective-permute-start.4
  155.5 8.7 %collective-permute-done.5 = bf16[1,256,1024]{2,1,0:T(8,128)(2,1)} collective-permute-done((bf16[1,256,1024]{2,1,0:T(8,128)(2,1)}, bf16[1,256,1024]{2,1,0:T(8,128)(2,1)}, u32[]{:S(2)}, u32[]{:S(2)}) %collective-permute-start.5) | collective-permute-done | bytes 524320 | tf_op jit(solution)/shard_map/ppermute | solution.py:25
  164.1 1.3 pad_maximum_fusion.1
  165.4 15.7 %collective-permute-done.4 = bf16[1,256,1024]{2,1,0:T(8,128)(2,1)S(1)} collective-permute-done((bf16[1,256,1024]{2,1,0:T(8,128)(2,1)}, bf16[1,256,1024]{2,1,0:T(8,128)(2,1)S(1)}, u32[]{:S(2)}, u32[]{:S(2)}) %collective-permute-start.4) | collective-permute-done | bytes 524320 | tf_op jit(solution)/shard_map/ppermute | solution.py:25
  181.2 0.8 copy-done.20
  182.0 1.3 pad_maximum_fusion
  183.3 1.2 reverse_select_fusion.2
  184.5 3.5 multiply_bitcast_fusion.2
  188.1 1.2 reverse_select_fusion.3
  189.3 10.4 %all-gather.9.cloned.1.call-done = bf16[512,1024]{1,0:T(8,128)(2,1)} async-done(((bf16[256,1024]{1,0:T(8,128)(2,1)}), bf16[512,1024]{1,0:T(8,128)(2,1)}) %all-gather.9.cloned.1.call-update) | async-done | bytes 1048592 | tf_op jit(solution)/shard_map/all_gather | solution.py:107
  199.6 2.3 multiply_bitcast_fusion.3
  201.9 1.3 copy-done.14
  203.3 5.8 %fusion = bf16[2,512,1024]{2,1,0:T(8,128)(2,1)} fusion(f32[2,512,1024]{2,1,0:T(8,128)S(1)} %copy-done.7, f32[1,512,1024]{2,1,0:T(8,128)} %multiply_bitcast_fusion.2, f32[1,512,1024]{2,1,0:T(8,128)S(1)} %multiply_bitcast_fusion.3, f32[2,512,1024]{2,1,0:T(8,128)} %param.6), kind=kLoop, calls=%fused_computation.12 | loop fusion | flops 6291456 | bytes 14680064 | tf_op jit(solution)/shard_map/convert_element_type | solution.py:89
  209.2 57.8 %all-gather.13.cloned.1.call-done = bf16[2,1024,1024]{2,1,0:T(8,128)(2,1)} async-done(((bf16[2,512,1024]{2,1,0:T(8,128)(2,1)}), bf16[2,1024,1024]{2,1,0:T(8,128)(2,1)}) %all-gather.13.cloned.1.call-update) | async-done | bytes 4194320 | tf_op jit(solution)/shard_map/all_gather | solution.py:89
  266.9 2.5 fusion.20
  269.7 0.8 fusion.17
  270.5 1.6 collective-permute-start.6
  272.2 2.2 collective-permute-done.6
  274.4 0.9 fusion.14
  275.2 0.8 fusion.11
  276.0 13.3 %collective-permute-start.7 = (f32[256,1024]{1,0:T(8,128)S(1)}, f32[256,1024]{1,0:T(8,128)S(1)}, u32[]{:S(2)}, u32[]{:S(2)}) collective-permute-start(f32[256,1024]{1,0:T(8,128)S(1)} %fusion.11), channel_id=1, source_target_pairs={{0,2},{2,4},{4,6},{6,8},{8,10},{10,12},{12,14},{14,16},{16,18},{18... | collective-permute-start | bytes 3145736 | tf_op jit(solution)/shard_map/ppermute | solution.py:39
  289.3 2.2 collective-permute-done.7
  291.6 1.1 fusion.84
  292.7 3.7 fusion.70
  296.3 3.3 add_subtract_fusion
  299.9 2.5 fusion.6
  302.4 0.8 fusion.5
  303.2 1.3 collective-permute-start.8
  304.5 14.7 %collective-permute-done.8 = f32[256,1024]{1,0:T(8,128)S(1)} collective-permute-done((f32[256,1024]{1,0:T(8,128)S(1)}, f32[256,1024]{1,0:T(8,128)S(1)}, u32[]{:S(2)}, u32[]{:S(2)}) %collective-permute-start.8) | collective-permute-done | bytes 1048608 | tf_op jit(solution)/shard_map/ppermute | solution.py:39
  319.2 0.8 fusion.4
  320.1 1.8 fusion.3
  321.9 1.3 collective-permute-start.9
  323.4 15.6 %collective-permute-done.9 = f32[256,1024]{1,0:T(8,128)} collective-permute-done((f32[256,1024]{1,0:T(8,128)}, f32[256,1024]{1,0:T(8,128)}, u32[]{:S(2)}, u32[]{:S(2)}) %collective-permute-start.9) | collective-permute-done | bytes 1048608 | tf_op jit(solution)/shard_map/ppermute | solution.py:39
  339.1 2.7 fusion.71
  342.3 2.3 fusion.42
  344.6 1.5 collective-permute-start.10
  346.2 10.1 %collective-permute-done.11 = bf16[1,256,1024]{2,1,0:T(8,128)(2,1)S(1)} collective-permute-done((bf16[1,256,1024]{2,1,0:T(8,128)(2,1)}, bf16[1,256,1024]{2,1,0:T(8,128)(2,1)S(1)}, u32[]{:S(2)}, u32[]{:S(2)}) %collective-permute-start.11) | collective-permute-done | bytes 524320 | tf_op jit(solution)/shard_map/ppermute | solution.py:25
  356.3 1.1 pad_maximum_fusion.3
  357.4 16.0 %collective-permute-done.10 = bf16[1,256,1024]{2,1,0:T(8,128)(2,1)S(1)} collective-permute-done((bf16[1,256,1024]{2,1,0:T(8,128)(2,1)S(1)}, bf16[1,256,1024]{2,1,0:T(8,128)(2,1)S(1)}, u32[]{:S(2)}, u32[]{:S(2)}) %collective-permute-start.10) | collective-permute-done | bytes 524320 | tf_op jit(solution)/shard_map/ppermute | solution.py:25
  373.8 3.1 multiply_bitcast_fusion
  376.9 1.2 reverse_select_fusion.1
  378.2 12.8 %all-gather.15.cloned.1.call-done = bf16[512,1024]{1,0:T(8,128)(2,1)} async-done(((bf16[256,1024]{1,0:T(8,128)(2,1)}), bf16[512,1024]{1,0:T(8,128)(2,1)}) %all-gather.15.cloned.1.call-update) | async-done | bytes 1048592 | tf_op jit(solution)/shard_map/all_gather | solution.py:107
  390.9 2.3 multiply_bitcast_fusion.1
  393.6 6.5 %multiply_subtract_fusion = (f32[2,512,1024]{2,1,0:T(8,128)}, f32[2,512,1024]{2,1,0:T(8,128)}) fusion(f32[2,512,1024]{2,1,0:T(8,128)S(1)} %copy-done.8, f32[1,512,1024]{2,1,0:T(8,128)S(1)} %copy-done.13, f32[1,512,1024]{2,1,0:T(8,128)} %copy-done.14, f32[2,512,1024]{2,1,0:T(8,128)} %param.6, f32[1,512,1024]{2,1,0:T(8,128)} %multiply_bitcast_fusion, ...), kind=kLoop, calls=%fused_computation.2 | loop fusion | flops 10485760 | bytes 25165824 | tf_op jit(solution)/shard_map/sub | solution.py:119
  (61 shorter events, 6.1 us)
Async XLA Ops:
  7.2 63.6 %copy-start.17 = (f32[1,256,1024]{2,1,0:T(8,128)S(1)}, f32[1,256,1024]{2,1,0:T(8,128)}, u32[]{:S(2)}) copy-start(f32[1,256,1024]{2,1,0:T(8,128)} %param.7) | copy-start | bytes 3145732
  7.2 63.6 %all-gather.7.cloned.1.call-start = ((), (), s32[]{:S(2)}) async-start(), calls=%async_computation | async-start | bytes 6291456 | tf_op jit(solution)/shard_map/all_gather | solution.py:89
  11.2 173.4 %all-gather.11.cloned.1.call-start = ((), (), s32[]{:S(2)}) async-start(), calls=%async_computation.2 | async-start | bytes 1572864 | tf_op jit(solution)/shard_map/all_gather | solution.py:107
  70.8 2.8 copy-start
  74.3 3.9 collective-permute-start
  76.0 5.0 %copy-start.1 = (bf16[2,1024,1024]{2,1,0:T(8,128)(2,1)S(1)}, bf16[2,1024,1024]{2,1,0:T(8,128)(2,1)}, u32[]{:S(2)}) copy-start(bf16[2,1024,1024]{2,1,0:T(8,128)(2,1)} %all-gather.7.cloned.1.call-done) | copy-start | bytes 12582916
  78.2 3.6 copy-start.19
  81.7 15.5 %collective-permute-start.1 = (f32[256,1024]{1,0:T(8,128)S(1)}, f32[256,1024]{1,0:T(8,128)S(1)}, u32[]{:S(2)}, u32[]{:S(2)}) collective-permute-start(f32[256,1024]{1,0:T(8,128)S(1)} %fusion.31), channel_id=1, source_target_pairs={{0,2},{2,4},{4,6},{6,8},{8,10},{10,12},{12,14},{14,16},{16,18},{18... | collective-permute-start | bytes 3145736 | tf_op jit(solution)/shard_map/ppermute | solution.py:39
  97.6 3.3 copy-start.15
  101.0 3.3 copy-start.2
  101.0 3.6 copy-start.18
  104.0 3.1 copy-start.11
  107.1 17.6 %collective-permute-start.2 = (f32[256,1024]{1,0:T(8,128)}, f32[256,1024]{1,0:T(8,128)}, u32[]{:S(2)}, u32[]{:S(2)}) collective-permute-start(f32[256,1024]{1,0:T(8,128)} %fusion.25), channel_id=1, source_target_pairs={{2,0},{4,2},{6,4},{8,6},{10,8},{12,10},{14,12},{16,14},{18,16},{20... | collective-permute-start | bytes 3145736 | tf_op jit(solution)/shard_map/ppermute | solution.py:39
  108.4 19.5 %copy-start.3 = (bf16[2,1024,1024]{2,1,0:T(8,128)(2,1)S(1)}, bf16[2,1024,1024]{2,1,0:T(8,128)(2,1)}, u32[]{:S(2)}) copy-start(bf16[2,1024,1024]{2,1,0:T(8,128)(2,1)} %all-gather.7.cloned.1.call-done) | copy-start | bytes 12582916
  129.7 17.2 %collective-permute-start.3 = (f32[256,1024]{1,0:T(8,128)}, f32[256,1024]{1,0:T(8,128)}, u32[]{:S(2)}, u32[]{:S(2)}) collective-permute-start(f32[256,1024]{1,0:T(8,128)} %fusion.23), channel_id=1, source_target_pairs={{2,0},{4,2},{6,4},{8,6},{10,8},{12,10},{14,12},{16,14},{18,16},{20... | collective-permute-start | bytes 3145736 | tf_op jit(solution)/shard_map/ppermute | solution.py:39
  131.0 68.7 %all-gather.9.cloned.1.call-start = ((), (), s32[]{:S(2)}) async-start(), calls=%async_computation.1 | async-start | bytes 1572864 | tf_op jit(solution)/shard_map/all_gather | solution.py:107
  149.5 14.6 %collective-permute-start.5 = (bf16[1,256,1024]{2,1,0:T(8,128)(2,1)}, bf16[1,256,1024]{2,1,0:T(8,128)(2,1)}, u32[]{:S(2)}, u32[]{:S(2)}) collective-permute-start(bf16[1,256,1024]{2,1,0:T(8,128)(2,1)} %bitcast.11), channel_id=1, source_target_pairs={{0,1},{1,0},{2,3},{3,2},{4,5},{5,4},{6,7},{7,6},{8,9},{9,8},{10,11... | collective-permute-start | bytes 1572872 | tf_op jit(solution)/shard_map/ppermute | solution.py:25
  153.8 27.4 %collective-permute-start.4 = (bf16[1,256,1024]{2,1,0:T(8,128)(2,1)}, bf16[1,256,1024]{2,1,0:T(8,128)(2,1)S(1)}, u32[]{:S(2)}, u32[]{:S(2)}) collective-permute-start(bf16[1,256,1024]{2,1,0:T(8,128)(2,1)} %bitcast.6), channel_id=1, source_target_pairs={{0,1},{1,0},{2,3},{3,2},{4,5},{5,4},{6,7},{7,6},{8,9},{9,8},{10,11... | collective-permute-start | bytes 1572872 | tf_op jit(solution)/shard_map/ppermute | solution.py:25
  155.2 111.7 %all-gather.13.cloned.1.call-start = ((), (), s32[]{:S(2)}) async-start(), calls=%async_computation.3 | async-start | bytes 6291456 | tf_op jit(solution)/shard_map/all_gather | solution.py:89
  181.2 0.8 copy-start.20
  199.6 3.6 copy-start.7
  201.9 1.4 copy-start.14
  203.3 63.7 %copy-start.16 = (bf16[256,1024]{1,0:T(8,128)(2,1)S(1)}, bf16[256,1024]{1,0:T(8,128)(2,1)}, u32[]{:S(2)}) copy-start(bf16[256,1024]{1,0:T(8,128)(2,1)} %copy-done.15) | copy-start | bytes 1572868
  209.1 164.7 %all-gather.17.cloned.1.call-start = ((), (), s32[]{:S(2)}) async-start(), calls=%async_computation.5 | async-start | bytes 1572864 | tf_op jit(solution)/shard_map/all_gather | solution.py:107
  266.9 2.8 copy-start.4
  270.5 3.9 collective-permute-start.6
  276.0 15.6 %collective-permute-start.7 = (f32[256,1024]{1,0:T(8,128)S(1)}, f32[256,1024]{1,0:T(8,128)S(1)}, u32[]{:S(2)}, u32[]{:S(2)}) collective-permute-start(f32[256,1024]{1,0:T(8,128)S(1)} %fusion.11), channel_id=1, source_target_pairs={{0,2},{2,4},{4,6},{6,8},{8,10},{10,12},{12,14},{14,16},{16,18},{18... | collective-permute-start | bytes 3145736 | tf_op jit(solution)/shard_map/ppermute | solution.py:39
  292.7 3.7 copy-start.12
  296.3 3.6 copy-start.5
  299.7 19.6 %copy-start.9 = (f32[256,1024]{1,0:T(8,128)}, f32[256,1024]{1,0:T(8,128)S(1)}, u32[]{:S(2)}) copy-start(f32[256,1024]{1,0:T(8,128)S(1)} %get-tuple-element.19) | copy-start | bytes 3145732
  303.2 16.0 %collective-permute-start.8 = (f32[256,1024]{1,0:T(8,128)S(1)}, f32[256,1024]{1,0:T(8,128)S(1)}, u32[]{:S(2)}, u32[]{:S(2)}) collective-permute-start(f32[256,1024]{1,0:T(8,128)S(1)} %fusion.5), channel_id=1, source_target_pairs={{2,0},{4,2},{6,4},{8,6},{10,8},{12,10},{14,12},{16,14},{18,16},{20... | collective-permute-start | bytes 3145736 | tf_op jit(solution)/shard_map/ppermute | solution.py:39
  320.1 19.0 %copy-start.10 = (f32[256,1024]{1,0:T(8,128)S(1)}, f32[256,1024]{1,0:T(8,128)}, u32[]{:S(2)}) copy-start(f32[256,1024]{1,0:T(8,128)} %copy-done.9) | copy-start | bytes 3145732
  321.9 17.2 %collective-permute-start.9 = (f32[256,1024]{1,0:T(8,128)}, f32[256,1024]{1,0:T(8,128)}, u32[]{:S(2)}, u32[]{:S(2)}) collective-permute-start(f32[256,1024]{1,0:T(8,128)} %fusion.3), channel_id=1, source_target_pairs={{2,0},{4,2},{6,4},{8,6},{10,8},{12,10},{14,12},{16,14},{18,16},{20... | collective-permute-start | bytes 3145736 | tf_op jit(solution)/shard_map/ppermute | solution.py:39
  323.2 67.8 %all-gather.15.cloned.1.call-start = ((), (), s32[]{:S(2)}) async-start(), calls=%async_computation.4 | async-start | bytes 1572864 | tf_op jit(solution)/shard_map/all_gather | solution.py:107
  323.4 18.9 %copy-start.6 = (bf16[2,1024,1024]{2,1,0:T(8,128)(2,1)S(1)}, bf16[2,1024,1024]{2,1,0:T(8,128)(2,1)}, u32[]{:S(2)}) copy-start(bf16[2,1024,1024]{2,1,0:T(8,128)(2,1)} %all-gather.13.cloned.1.call-done) | copy-start | bytes 12582916
  341.8 14.5 %collective-permute-start.11 = (bf16[1,256,1024]{2,1,0:T(8,128)(2,1)}, bf16[1,256,1024]{2,1,0:T(8,128)(2,1)S(1)}, u32[]{:S(2)}, u32[]{:S(2)}) collective-permute-start(bf16[1,256,1024]{2,1,0:T(8,128)(2,1)} %bitcast.23), channel_id=1, source_target_pairs={{0,1},{1,0},{2,3},{3,2},{4,5},{5,4},{6,7},{7,6},{8,9},{9,8},{10,11... | collective-permute-start | bytes 1572872 | tf_op jit(solution)/shard_map/ppermute | solution.py:25
  344.6 28.8 %collective-permute-start.10 = (bf16[1,256,1024]{2,1,0:T(8,128)(2,1)S(1)}, bf16[1,256,1024]{2,1,0:T(8,128)(2,1)S(1)}, u32[]{:S(2)}, u32[]{:S(2)}) collective-permute-start(bf16[1,256,1024]{2,1,0:T(8,128)(2,1)S(1)} %bitcast.98), channel_id=1, source_target_pairs={{0,1},{1,0},{2,3},{3,2},{4,5},{5,4},{6,7},{7,6},{8,9},{9,8},{10,11... | collective-permute-start | bytes 1572872 | tf_op jit(solution)/shard_map/ppermute | solution.py:25
  376.9 16.3 %copy-start.13 = (f32[1,512,1024]{2,1,0:T(8,128)S(1)}, f32[1,512,1024]{2,1,0:T(8,128)}, u32[]{:S(2)}) copy-start(f32[1,512,1024]{2,1,0:T(8,128)} %multiply_bitcast_fusion.2) | copy-start | bytes 6291460
  390.9 2.7 copy-start.8
Sparse Core Ops, SparseCore 0:
  11.3 59.4 all-gather.6
  131.1 45.2 all-gather.10
  178.0 21.6 all-gather.8
  209.2 57.6 all-gather.12
  323.3 45.3 all-gather.16
  370.0 20.8 all-gather.14
